TPU v7x, 512 devices: a whole 4x8x8 slice. The times are simulated.
512 devices in a mesh: sub: 4 (over z_lo), row: 16 (over z_hi, x, core), col: 8 (over y).
Axes of the slice: x: 4, y: 8, z: 8 (z_hi: 2, z_lo: 4; z = z_hi * 4 + z_lo), core: 2. Of those that a mesh axis runs over, the one named last changes fastest.
Arguments:
- child_update: bfloat16 [32768, 8192], P(('sub', 'row'), 'col'), may hold values from -2.8 to 2.8, as said below
- parent_front: bfloat16 [16384, 16384], P('row', ('sub', 'col')), may hold values from -2.8 to 256, as said below
- tile_map: int32 [4, 64], replicated, may hold values from -1 to 127, as said below
Outputs:
- front_out: float32 [16384, 16384], P('row', ('sub', 'col'))
Inputs may be any that keep to these rules, and one draw needn't show every extreme that they name: Live tiles of a child come first, a whole multiple of 16 of them, at least max(1, 2) * 16; then -1. At least one child has all 64 tiles live. Within one child the parent tiles are distinct, and (tile_map[s, j] // 4) % 16 == j % 16 for every live j. `child_update`: each child's update, in logical order, is a symmetric matrix. `parent_front`: symmetric in logical order, with diagonal entries between 64 and 256; the assembled leading 4 x 4 tiles are positive definite.
All inputs are finite; a program needn't handle non-finite values.
Results may differ from a plain program's by a relative error of at most 0.0008.
Values may be sent and summed in bfloat16 or wider, within the bound.
A program may use at most 64 MiB of HBM per device.

v0:
```python
import jax
import jax.numpy as jnp
from jax import lax
from jax.sharding import PartitionSpec as P

TILE = 128
PANEL = 4
precise = lax.Precision.HIGHEST


def from_root(x, axis, root):
    mine = lax.axis_index(axis) == root
    return lax.psum(jnp.where(mine, x, jnp.zeros_like(x)), axis)


def body(child_update, parent_front, tile_map):
    tile_len = TILE
    panel_tiles = PANEL
    panel_width = panel_tiles * tile_len
    sub_count = lax.axis_size("sub")
    row_count = lax.axis_size("row")
    col_count = lax.axis_size("col")
    sub_id = lax.axis_index("sub")
    row_id = lax.axis_index("row")
    col_id = lax.axis_index("col")
    block_id = sub_id * col_count + col_id
    child_rows = child_update.shape[0] // tile_len
    child_cols = child_update.shape[1] // tile_len
    front_rows = parent_front.shape[0] // tile_len
    own_map = lax.dynamic_index_in_dim(tile_map, sub_id, 0, keepdims=False)
    own_cols = lax.dynamic_index_in_dim(
        own_map.reshape(child_cols, col_count), col_id, 1, keepdims=False
    )
    live_cols = own_cols >= 0
    destination = jnp.floor_divide(jnp.floor_divide(own_cols, panel_tiles), col_count)
    slot_index = jnp.remainder(own_cols, panel_tiles)
    dest_hit = destination[None, :] == jnp.arange(sub_count, dtype=jnp.int32)[:, None]
    slot_hit = slot_index[None, :] == jnp.arange(panel_tiles, dtype=jnp.int32)[:, None]
    select = (live_cols[None, None, :] & dest_hit[:, None, :] & slot_hit[None, :, :]).astype(
        jnp.bfloat16
    )
    column_slabs = child_update.reshape(child_rows * tile_len, child_cols, tile_len)
    payload = jnp.einsum(
        "dqk,rky->dqry", select, column_slabs, preferred_element_type=jnp.float32
    ).astype(jnp.bfloat16)
    maps_rows = lax.dynamic_index_in_dim(
        tile_map.reshape(sub_count, child_rows, row_count), row_id, 2, keepdims=False
    )
    local_row = jnp.floor_divide(
        jnp.floor_divide(maps_rows, panel_tiles), row_count
    ) * panel_tiles + jnp.remainder(maps_rows, panel_tiles)
    row_hit = (maps_rows[:, :, None] >= 0) & (
        local_row[:, :, None] == jnp.arange(front_rows, dtype=jnp.int32)[None, None, :]
    )
    place_row = row_hit.astype(jnp.bfloat16)
    arrived = lax.all_to_all(payload, "sub", split_axis=0, concat_axis=0, tiled=True)
    slot_count = arrived.shape[1]
    grid = arrived.reshape(sub_count, slot_count, child_rows, tile_len, tile_len)
    spread = jnp.einsum("ska,sqkyx->ayqx", place_row, grid, preferred_element_type=jnp.float32)
    placed = spread.reshape(front_rows * tile_len, slot_count * tile_len)
    front_local = parent_front.astype(jnp.float32) + placed
    top_block = from_root(front_local[:panel_width].astype(jnp.bfloat16), "row", 0).astype(
        jnp.float32
    )
    panel_rows, leading = (
        from_root(front_local.astype(jnp.bfloat16), ("sub", "col"), 0).astype(front_local.dtype),
        from_root(top_block.astype(jnp.bfloat16), ("sub", "col"), 0).astype(top_block.dtype),
    )
    lower_factor = jnp.tril(jnp.linalg.cholesky(leading))
    identity = jnp.eye(panel_width, dtype=jnp.float32)
    inverse = jax.scipy.linalg.solve_triangular(lower_factor, identity, lower=True)
    factor_rows = jnp.dot(
        panel_rows, inverse.T, precision=precise, preferred_element_type=jnp.float32
    )
    head_rows = jnp.where(row_id == 0, lower_factor, factor_rows[:panel_width])
    factor_rows = jnp.concatenate([head_rows, factor_rows[panel_width:]], axis=0)
    source_row = jnp.remainder(block_id, row_count)
    first_row = jnp.floor_divide(block_id, row_count) * panel_width
    factor_piece = lax.dynamic_slice_in_dim(factor_rows, first_row, panel_width, 0)
    column_side = from_root(factor_piece.astype(jnp.bfloat16), "row", source_row).astype(
        factor_piece.dtype
    )
    update = jnp.dot(
        factor_rows, column_side.T, precision=precise, preferred_element_type=jnp.float32
    )
    keep_rows = (jnp.arange(front_rows * tile_len) >= panel_width) | (row_id != 0)
    trailing = front_local - jnp.where(keep_rows[:, None], update, 0.0)
    return jnp.where(block_id == 0, factor_rows, trailing)


def solution(mesh):
    in_specs = (P(("sub", "row"), "col"), P("row", ("sub", "col")), P())
    out_specs = P("row", ("sub", "col"))
    return jax.shard_map(body, mesh=mesh, in_specs=in_specs, out_specs=out_specs, check_vma=False)
```

profile of v0, /device:TPU:1, one launch (start us, length us, event | category | flops | bytes accessed | tf_op | source)
XLA Modules:
  0.0 940.0 jit_solution(14643982582038537792)
XLA Ops:
  6.5 0.7 fusion.65
  7.5 1.5 copy.51
  9.1 2.0 convolution_convert_fusion
  11.1 7.9 all-to-all-start
  19.5 1.5 copy.23
  21.0 45.7 %all-to-all-done = bf16[4,4,512,128]{3,1,2,0:T(4,128)(2,1)S(1)} async-done(((bf16[4,4,512,128]{3,1,2,0:T(4,128)(2,1)}), bf16[4,4,512,128]{3,1,2,0:T(4,128)(2,1)S(1)}, u32[]{:S(2)}, u32[]{:S(2)}) %all-to-all-start) | async-done | bytes 2097184 | tf_op jit(solution)/shard_map/all_to_all | solution.py:56
  66.8 5.0 fusion.3
  71.8 2.0 copy.28
  73.8 1.7 broadcast_select_fusion
  75.6 0.8 slice_select_fusion.1
  76.5 187.6 %all-reduce.6.cloned.1.call-done = bf16[512,512]{0,1:T(8,128)(2,1)} async-done(((bf16[512,512]{0,1:T(8,128)(2,1)}), bf16[512,512]{0,1:T(8,128)(2,1)}) %all-reduce.6.cloned.1.call-update) | async-done | bytes 524304 | tf_op jit(solution)/shard_map/psum | solution.py:13
  264.0 1.9 broadcast_select_fusion.1
  265.9 0.5 all-reduce.8.cloned.1.call-start
  266.5 0.8 iota_compare_fusion
  267.3 1.2 fusion.28
  268.4 290.1 %all-reduce.10.cloned.1.call-done = (bf16[512,512]{0,1:T(8,128)(2,1)}, bf16[1024,512]{0,1:T(8,128)(2,1)}) async-done(((bf16[512,512]{0,1:T(8,128)(2,1)}, bf16[1024,512]{0,1:T(8,128)(2,1)}), (bf16[512,512]{0,1:T(8,128)(2,1)}, bf16[1024,512]{0,1:T(8,128)(2,1)})) %all-reduce.10.cloned.1.call-update) | async-done | bytes 1572880 | tf_op jit(solution)/shard_map/psum | solution.py:13
  558.5 1.3 copy.29
  559.7 1.2 fusion.17
  560.9 1.0 copy-done.4
  561.9 11.7 %cholesky.104 = f32[128,128]{1,0:T(8,128)S(1)} custom-call(f32[128,128]{1,0:T(8,128)S(1)} %cholesky.266), custom_call_target="Cholesky" | custom-call | tf_op jit(solution)/shard_map/jit(cholesky)/cholesky | solution.py:69
  573.6 0.7 copy.30
  574.4 9.8 %custom-call.31 = f32[1,128,128]{1,2,0:T(8,128)S(1)} custom-call(f32[1,128,128]{2,1,0:T(8,128)S(1)} %get-tuple-element.42), custom_call_target="InvertDiagBlocksLowerTriangular" | custom-call | tf_op jit(solution)/shard_map/jit(cholesky)/cholesky | solution.py:69
  584.2 1.2 fusion.34
  585.6 1.3 convolution_subtract_fusion.3
  586.9 11.7 %cholesky.217 = f32[128,128]{1,0:T(8,128)S(1)} custom-call(f32[128,128]{1,0:T(8,128)S(1)} %cholesky.270), custom_call_target="Cholesky" | custom-call | tf_op jit(solution)/shard_map/jit(cholesky)/cholesky | solution.py:69
  598.6 0.7 copy.32
  599.3 10.6 %custom-call.32 = f32[1,128,128]{1,2,0:T(8,128)} custom-call(f32[1,128,128]{2,1,0:T(8,128)S(1)} %get-tuple-element.40), custom_call_target="InvertDiagBlocksLowerTriangular" | custom-call | tf_op jit(solution)/shard_map/jit(cholesky)/cholesky | solution.py:69
  609.9 1.0 cholesky.224
  610.9 0.8 constant_dynamic-update-slice_fusion.3
  611.7 1.2 convolution_dynamic-update-slice_fusion
  612.9 1.5 convolution_subtract_fusion.4
  614.4 11.7 %cholesky.238 = f32[128,128]{1,0:T(8,128)S(1)} custom-call(f32[128,128]{1,0:T(8,128)S(1)} %cholesky.275), custom_call_target="Cholesky" | custom-call | tf_op jit(solution)/shard_map/jit(cholesky)/cholesky | solution.py:69
  626.3 9.8 %custom-call.33 = f32[1,128,128]{1,2,0:T(8,128)S(1)} custom-call(f32[1,128,128]{2,1,0:T(8,128)S(1)} %get-tuple-element.38), custom_call_target="InvertDiagBlocksLowerTriangular" | custom-call | tf_op jit(solution)/shard_map/jit(cholesky)/cholesky | solution.py:69
  636.4 1.3 convolution_subtract_fusion.5
  637.7 11.9 %cholesky.255 = f32[128,128]{1,0:T(8,128)S(1)} custom-call(f32[128,128]{1,0:T(8,128)S(1)} %convolution_subtract_fusion.5), custom_call_target="Cholesky" | custom-call | tf_op jit(solution)/shard_map/jit(cholesky)/cholesky | solution.py:69
  649.8 0.7 compare_reduce_fusion.3
  650.5 0.7 compare_reduce_fusion.2
  651.2 0.7 compare_reduce_fusion.1
  651.9 0.6 compare_reduce_fusion
  655.1 1.1 fusion.18
  656.2 14.7 %while.1 = (s32[]{:T(128)}, f32[512,512]{0,1:T(8,128)}, s32[4,2]{0,1:T(2,128)S(1)}, f32[4,128,128]{2,1,0:T(8,128)}, s32[]{:T(128)}) while((s32[]{:T(128)}, f32[512,512]{0,1:T(8,128)}, s32[4,2]{0,1:T(2,128)S(1)}, f32[4,128,128]{2,1,0:T(8,128)}, s32[]{:T(128)}) %tuple.28), condition=%wide.while_cond, body=%wide.while_body.sunk | while | flops 2 | bytes 393329 | solution.py:71
  656.3 0.6 fusion.81
  656.8 2.3 dynamic-slice.7
  659.2 0.6 bitcast_dynamic-update-slice_fusion.2
  659.9 0.6 fusion.81
  660.5 2.3 dynamic-slice.7
  662.9 0.6 bitcast_dynamic-update-slice_fusion.2
  663.6 0.6 fusion.81
  664.2 2.3 dynamic-slice.7
  666.6 0.6 bitcast_dynamic-update-slice_fusion.2
  667.3 0.6 fusion.81
  667.9 2.2 dynamic-slice.7
  670.2 0.6 bitcast_dynamic-update-slice_fusion.2
  670.9 40.1 %custom-call.34 = f32[4,128,128]{1,2,0:T(8,128)S(1)} custom-call(f32[4,128,128]{2,1,0:T(8,128)} %get-tuple-element.12), custom_call_target="InvertDiagBlocksLowerTriangular" | custom-call | tf_op jit(solution)/shard_map/jit(_solve_triangular)/triangular_solve | solution.py:71
  711.0 1.1 fusion.30
  712.1 1.4 convolution_subtract_fusion.1
  714.0 1.5 convolution_subtract_fusion
  715.9 1.7 convolution_subtract_fusion.2
  718.1 1.8 fusion.9
  720.2 1.0 copy-done
  721.2 1.1 fusion.24
  722.3 202.5 %all-reduce.8.cloned.1.call-done = bf16[512,512]{0,1:T(8,128)(2,1)} async-done(((bf16[512,512]{0,1:T(8,128)(2,1)}), bf16[512,512]{0,1:T(8,128)(2,1)}) %all-reduce.8.cloned.1.call-update) | async-done | bytes 524304 | tf_op jit(solution)/shard_map/psum | solution.py:13
  924.8 5.6 subtract_select_fusion
  930.4 2.9 copy.41
  (59 shorter events, 3.9 us)
Async XLA Ops:
  11.1 7.9 copy-start.6
  11.1 55.7 %all-to-all-start = ((bf16[4,4,512,128]{3,1,2,0:T(4,128)(2,1)}), bf16[4,4,512,128]{3,1,2,0:T(4,128)(2,1)S(1)}, u32[]{:S(2)}, u32[]{:S(2)}) async-start(bf16[4,4,512,128]{3,1,2,0:T(4,128)(2,1)} %convolution_convert_fusion), calls=%async_computation | async-start | bytes 4194304 | tf_op jit(solution)/shard_map/all_to_all | solution.py:56
  19.0 245.0 %all-reduce.6.cloned.1.call-start = ((), (), s32[]{:S(2)}) async-start(), calls=%async_computation.1 | async-start | bytes 1048576 | tf_op jit(solution)/shard_map/psum | solution.py:13
  21.0 52.8 %copy-start.3 = (bf16[1024,512]{0,1:T(8,128)(2,1)}, bf16[1024,512]{0,1:T(8,128)(2,1)S(1)}, u32[]{:S(2)}) copy-start(bf16[1024,512]{0,1:T(8,128)(2,1)S(1)} %copy.23) | copy-start | bytes 3145732
  76.4 482.0 %all-reduce.10.cloned.1.call-start = ((), (), s32[]{:S(2)}) async-start(), calls=%async_computation.3 | async-start | bytes 3145728 | tf_op jit(solution)/shard_map/psum | solution.py:13
  265.9 658.8 %all-reduce.8.cloned.1.call-start = ((), (), s32[]{:S(2)}) async-start(), calls=%async_computation.2 | async-start | bytes 1048576 | tf_op jit(solution)/shard_map/psum | solution.py:13
  560.9 1.0 copy-start.4
  649.8 6.4 copy-start.1
  713.5 4.5 copy-start.5
  718.1 1.8 copy-start.2
  720.2 1.0 copy-start
Sparse Core Ops, SparseCore 0:
  76.5 187.4 all-reduce.5
  267.0 291.4 all-reduce.9
  722.4 202.3 all-reduce.7
where the time goes:
time: 946 us; the launch traced here: 940 us
  waiting for transfers between devices  726 us (77%)
  other arithmetic  130 us (14%)
  local copies, waits for them, and re-layouts  30.8 us (3%)
  matrix products  28.2 us (3%)
  between operations  16.3 us (2%)
    psum x3, waiting for transfers between devices, from_root(): return lax.psum(jnp.where(mine, x, jnp.zeros_like(x)), axis)  680 us
    another operation x15, other arithmetic, body(): lower_factor = jnp.tril(jnp.linalg.cholesky(leading))  80.1 us
    all_to_all x1, waiting for transfers between devices, body(): lax.all_to_all(payload, 'sub', split_axis=0, concat_axis=0, tiled=True)  45.7 us
    another operation x3, other arithmetic, body(): jax.scipy.linalg.solve_triangular(lower_factor, identity, lower=True)  41.2 us
  transfers between devices with their start and end apart: 4, of which 4 were waited for; matrix products, arithmetic and copies ran while one was open for 0% of the time, Pallas kernels for 0%

commit v1 on v0

--- a/solution.py
+++ b/solution.py
@@ -10,7 +10,7 @@
 
 def from_root(x, axis, root):
     mine = lax.axis_index(axis) == root
-    return lax.psum(jnp.where(mine, x, jnp.zeros_like(x)), axis)
+    return jnp.sum(lax.all_gather(jnp.where(mine, x, jnp.zeros_like(x)), axis), axis=0)
 
 
 def body(child_update, parent_front, tile_map):

time: 946 us -> 909 us (0.961)
  waiting for transfers between devices: 726 us -> 668 us
  other arithmetic: 130 us -> 160 us
  local copies, waits for them, and re-layouts: 30.8 us -> 21.3 us
    psum x3 -> x0, waiting for transfers between devices: 680 us -> none  [from_root(): return lax.psum(jnp.where(mine, x, jnp.zeros_like(x)), axis)]
    all_gather x0 -> x4, waiting for transfers between devices: none -> 620 us  [from_root(): lax.all_gather(jnp.where(mine, x, jnp.zeros_like(x)), axis)]
    reduce_sum x0 -> x4, other arithmetic: none -> 31 us  [from_root(): jnp.sum(lax.all_gather(jnp.where(mine, x, jnp.zeros_like(x)), axis), axis=0)]
  transfers between devices with their start and end apart: 4 -> 5, of which waited for: 4 -> 5; matrix products, arithmetic and copies ran while one was open for 0% -> 18% of each run, Pallas kernels for 0% -> 0%
where the time goes in v1:
time: 909 us; the launch traced here: 902 us
  waiting for transfers between devices  668 us (73%)
  other arithmetic  160 us (18%)
  matrix products  28.4 us (3%)
  local copies, waits for them, and re-layouts  21.3 us (2%)
  between operations  16 us (2%)
    all_gather x4, waiting for transfers between devices, from_root(): lax.all_gather(jnp.where(mine, x, jnp.zeros_like(x)), axis)  620 us
    another operation x15, other arithmetic, body(): lower_factor = jnp.tril(jnp.linalg.cholesky(leading))  79.4 us
    all_to_all x1, waiting for transfers between devices, body(): lax.all_to_all(payload, 'sub', split_axis=0, concat_axis=0, tiled=True)  47.2 us
    another operation x3, other arithmetic, body(): jax.scipy.linalg.solve_triangular(lower_factor, identity, lower=True)  41.9 us
    reduce_sum x4, other arithmetic, from_root(): jnp.sum(lax.all_gather(jnp.where(mine, x, jnp.zeros_like(x)), axis), axis=0)  31 us
  transfers between devices with their start and end apart: 5, of which 5 were waited for; matrix products, arithmetic and copies ran while one was open for 18% of the time, Pallas kernels for 0%

profile of v1, /device:TPU:1, one launch (start us, length us, event | category | flops | bytes accessed | tf_op | source)
XLA Modules:
  0.0 901.6 jit_solution(17305398417554603714)
XLA Ops:
  6.5 0.7 fusion.65
  7.5 1.5 copy.27
  9.1 2.0 convolution_convert_fusion
  11.1 7.9 all-to-all-start
  19.5 47.2 %all-to-all-done = bf16[4,4,512,128]{3,1,2,0:T(4,128)(2,1)S(1)} async-done(((bf16[4,4,512,128]{3,1,2,0:T(4,128)(2,1)}), bf16[4,4,512,128]{3,1,2,0:T(4,128)(2,1)S(1)}, u32[]{:S(2)}, u32[]{:S(2)}) %all-to-all-start) | async-done | bytes 2097184 | tf_op jit(solution)/shard_map/all_to_all | solution.py:56
  66.8 3.7 fusion.3
  70.5 1.4 copy.20
  71.8 1.4 broadcast_select_fusion
  73.3 0.9 slice_select_fusion.1
  74.2 117.2 %all-gather.9.cloned.1.call-done = bf16[8192,512]{1,0:T(8,128)(2,1)} async-done(((bf16[512,512]{1,0:T(8,128)(2,1)}), bf16[8192,512]{1,0:T(8,128)(2,1)}) %all-gather.9.cloned.1.call-update) | async-done | bytes 8388624 | tf_op jit(solution)/shard_map/all_gather | solution.py:13
  191.4 4.8 reduce_sum.48
  196.2 0.8 broadcast_select_fusion.1
  197.1 0.7 all-gather.13.cloned.1.call-update
  197.9 0.8 iota_compare_fusion
  198.7 1.1 fusion.28
  199.8 188.2 %all-gather.11.cloned.1.call-done = bf16[16384,512]{1,0:T(8,128)(2,1)} async-done(((bf16[512,512]{1,0:T(8,128)(2,1)}), bf16[16384,512]{1,0:T(8,128)(2,1)}) %all-gather.11.cloned.1.call-update) | async-done | bytes 16777232 | tf_op jit(solution)/shard_map/all_gather | solution.py:13
  388.0 9.3 %reduce_sum.49 = bf16[512,512]{1,0:T(8,128)(2,1)S(1)} reduce(bf16[32,512,512]{2,1,0:T(8,128)(2,1)} %bitcast.91, bf16[]{:T(256)} %constant.264.clone.1), dimensions={0}, to_apply=%region_1.2 | reduce | flops 8126464 | bytes 17301506 | tf_op jit(solution)/shard_map/reduce_sum | solution.py:13
  397.5 1.2 copy.22
  398.7 1.4 fusion.17
  400.1 1.0 copy-done.5
  401.1 11.7 %cholesky.104 = f32[128,128]{1,0:T(8,128)S(1)} custom-call(f32[128,128]{1,0:T(8,128)S(1)} %cholesky.266), custom_call_target="Cholesky" | custom-call | tf_op jit(solution)/shard_map/jit(cholesky)/cholesky | solution.py:69
  412.9 9.8 %custom-call.31 = f32[1,128,128]{1,2,0:T(8,128)S(1)} custom-call(f32[1,128,128]{2,1,0:T(8,128)S(1)} %get-tuple-element.36), custom_call_target="InvertDiagBlocksLowerTriangular" | custom-call | tf_op jit(solution)/shard_map/jit(cholesky)/cholesky | solution.py:69
  422.7 1.2 constant_dynamic-update-slice_fusion
  424.0 1.3 convolution_subtract_fusion.3
  425.3 11.7 %cholesky.217 = f32[128,128]{1,0:T(8,128)S(1)} custom-call(f32[128,128]{1,0:T(8,128)S(1)} %cholesky.270), custom_call_target="Cholesky" | custom-call | tf_op jit(solution)/shard_map/jit(cholesky)/cholesky | solution.py:69
  437.0 10.0 %custom-call.32 = f32[1,128,128]{1,2,0:T(8,128)S(1)} custom-call(f32[1,128,128]{2,1,0:T(8,128)S(1)} %get-tuple-element.33), custom_call_target="InvertDiagBlocksLowerTriangular" | custom-call | tf_op jit(solution)/shard_map/jit(cholesky)/cholesky | solution.py:69
  447.0 0.3 convolution_dynamic-update-slice_fusion
  447.3 1.3 convolution_subtract_fusion.4
  448.6 11.7 %cholesky.238 = f32[128,128]{1,0:T(8,128)S(1)} custom-call(f32[128,128]{1,0:T(8,128)S(1)} %cholesky.275), custom_call_target="Cholesky" | custom-call | tf_op jit(solution)/shard_map/jit(cholesky)/cholesky | solution.py:69
  460.3 9.8 %custom-call.33 = f32[1,128,128]{1,2,0:T(8,128)S(1)} custom-call(f32[1,128,128]{2,1,0:T(8,128)S(1)} %get-tuple-element.30), custom_call_target="InvertDiagBlocksLowerTriangular" | custom-call | tf_op jit(solution)/shard_map/jit(cholesky)/cholesky | solution.py:69
  470.4 1.2 convolution_subtract_fusion.5
  471.6 11.7 %cholesky.255 = f32[128,128]{1,0:T(8,128)S(1)} custom-call(f32[128,128]{1,0:T(8,128)S(1)} %convolution_subtract_fusion.5), custom_call_target="Cholesky" | custom-call | tf_op jit(solution)/shard_map/jit(cholesky)/cholesky | solution.py:69
  483.3 0.6 compare_reduce_fusion.3
  483.9 0.6 compare_reduce_fusion.2
  485.7 0.6 compare_reduce_fusion.1
  486.9 0.2 select_reduce_fusion
  487.1 0.7 compare_reduce_fusion
  488.5 1.1 fusion.18
  489.6 13.4 %while.1 = (s32[]{:T(128)}, f32[512,512]{1,0:T(8,128)}, s32[4,2]{0,1:T(2,128)S(1)}, f32[4,128,128]{2,1,0:T(8,128)}, s32[]{:T(128)}) while((s32[]{:T(128)}, f32[512,512]{1,0:T(8,128)}, s32[4,2]{0,1:T(2,128)S(1)}, f32[4,128,128]{2,1,0:T(8,128)}, s32[]{:T(128)}) %tuple.30), condition=%wide.while_cond, body=%wide.while_body.sunk | while | flops 2 | bytes 132205 | solution.py:71
  489.7 0.5 fusion.81
  490.2 2.8 bitcast_dynamic-update-slice_fusion.2
  493.0 0.5 fusion.81
  493.6 2.8 bitcast_dynamic-update-slice_fusion.2
  496.4 0.5 fusion.81
  496.9 2.8 bitcast_dynamic-update-slice_fusion.2
  499.8 0.5 fusion.81
  500.3 2.7 bitcast_dynamic-update-slice_fusion.2
  503.0 40.7 %custom-call.34 = f32[4,128,128]{1,2,0:T(8,128)} custom-call(f32[4,128,128]{2,1,0:T(8,128)} %get-tuple-element.12), custom_call_target="InvertDiagBlocksLowerTriangular" | custom-call | tf_op jit(solution)/shard_map/jit(_solve_triangular)/triangular_solve | solution.py:71
  543.7 1.2 fusion.30
  544.9 1.4 convolution_subtract_fusion.1
  546.3 1.3 fusion.42
  547.6 1.5 convolution_subtract_fusion
  549.2 0.4 fusion.40
  549.6 1.8 convolution_subtract_fusion.2
  551.4 1.1 fusion.39
  552.5 203.7 %all-gather.13.cloned.1.call-done = bf16[32768,512]{1,0:T(8,128)(2,1)} async-done(((bf16[1024,512]{1,0:T(8,128)(2,1)}), bf16[32768,512]{1,0:T(8,128)(2,1)}) %all-gather.13.cloned.1.call-update) | async-done | bytes 33554448 | tf_op jit(solution)/shard_map/all_gather | solution.py:13
  756.2 11.4 %reduce_sum.50 = bf16[1024,512]{1,0:T(8,128)(2,1)S(1)} reduce(bf16[32,1024,512]{2,1,0:T(8,128)(2,1)} %bitcast.88, bf16[]{:T(256)} %constant.264.clone.1), dimensions={0}, to_apply=%region_10.11 | reduce | flops 16252928 | bytes 34603008 | tf_op jit(solution)/shard_map/reduce_sum | solution.py:13
  767.6 3.1 fusion.9
  770.7 0.3 slice_select_fusion
  771.0 1.1 copy-done
  772.1 1.3 fusion.24
  773.4 110.6 %all-gather.15.cloned.1.call-done = bf16[8192,512]{1,0:T(8,128)(2,1)} async-done(((bf16[512,512]{1,0:T(8,128)(2,1)}), bf16[8192,512]{1,0:T(8,128)(2,1)}) %all-gather.15.cloned.1.call-update) | async-done | bytes 8388624 | tf_op jit(solution)/shard_map/all_gather | solution.py:13
  883.9 5.5 reduce_sum.51
  889.4 5.4 subtract_select_fusion
  (52 shorter events, 2.0 us)
Async XLA Ops:
  11.1 7.9 copy-start.8
  11.1 55.7 %all-to-all-start = ((bf16[4,4,512,128]{3,1,2,0:T(4,128)(2,1)}), bf16[4,4,512,128]{3,1,2,0:T(4,128)(2,1)S(1)}, u32[]{:S(2)}, u32[]{:S(2)}) async-start(bf16[4,4,512,128]{3,1,2,0:T(4,128)(2,1)} %convolution_convert_fusion), calls=%async_computation | async-start | bytes 4194304 | tf_op jit(solution)/shard_map/all_to_all | solution.py:56
  19.0 172.4 %all-gather.9.cloned.1.call-start = ((), (), s32[]{:S(2)}) async-start(), calls=%async_computation.1 | async-start | bytes 8912896 | tf_op jit(solution)/shard_map/all_gather | solution.py:13
  70.5 1.4 copy-start.4
  74.2 313.8 %all-gather.11.cloned.1.call-start = ((), (), s32[]{:S(2)}) async-start(), calls=%async_computation.2 | async-start | bytes 17301504 | tf_op jit(solution)/shard_map/all_gather | solution.py:13
  197.1 559.1 %all-gather.13.cloned.1.call-start = ((), (), s32[]{:S(2)}) async-start(), calls=%async_computation.3 | async-start | bytes 34603008 | tf_op jit(solution)/shard_map/all_gather | solution.py:13
  197.8 686.1 %all-gather.15.cloned.1.call-start = ((), (), s32[]{:S(2)}) async-start(), calls=%async_computation.4 | async-start | bytes 8912896 | tf_op jit(solution)/shard_map/all_gather | solution.py:13
  400.1 1.0 copy-start.5
  487.1 59.2 %copy-start.1 = (f32[512,512]{1,0:T(8,128)}, f32[512,512]{1,0:T(8,128)S(1)}, u32[]{:S(2)}) copy-start(f32[512,512]{1,0:T(8,128)S(1)} %get-tuple-element.28) | copy-start | bytes 3145732
  543.7 5.4 copy-start.7
  547.6 2.0 copy-start.3
  549.6 1.8 copy-start.6
  767.6 3.1 copy-start.2
  771.0 1.1 copy-start
Sparse Core Ops, SparseCore 0:
  74.3 117.0 all-gather.8
  197.2 190.7 all-gather.10
  390.1 366.0 all-gather.12
  773.5 110.4 all-gather.14
